TPU v7x, 256 devices: a whole 4x4x8 slice. The times are simulated.
256 devices in a mesh: pool: 8 (over z), tp: 32 (over x, y, core).
Axes of the slice: x: 4, y: 4, z: 8, core: 2. Of those that a mesh axis runs over, the one named last changes fastest.
Arguments:
- tokens: bfloat16 [4096, 8192], P(('pool', 'tp')), may hold values from -4 to 4
- lengths: int32 [8, 4], P('pool'), may hold values from 1 to 256, 512 in all within a row
- hit_pages: int32 [8, 4, 4], P('pool'), may hold values from 0 to 4095, as said below
- new_owner: int32 [8, 16], P('pool'), may hold values from 0 to 7, as said below
- w_query: bfloat16 [8192, 8192], P('pool', 'tp'), may hold values from -0.125 to 0.125
- w_keyval: bfloat16 [4096, 4096], P('pool', 'tp'), may hold values from -0.0625 to 0.0625
- w_out: bfloat16 [8192, 8192], P('tp', 'pool'), may hold values from -0.0625 to 0.0625
- pool_pages: bfloat16 [4096, 32, 2048], P('pool', 'tp'), may hold values from -65 to 65
Outputs:
- mixed: float32 [4096, 8192], P(('pool', 'tp'))
- new_store: bfloat16 [128, 32, 2048], P('pool', 'tp')
Inputs may be any that keep to these rules, and one draw needn't show every extreme that they name: Page p of the pool lies on pool index p // 512. In every group g at most 6 of the 16 entries of hit_pages[g] lie on one pool index, and some pool index holds exactly 6 of them in every group. A page may appear more than once. `new_owner`: in every group at most 2 of its 16 pages go to one pool index, and some pool index receives exactly 2 from every group. Row g holds the lengths of the 4 requests packed in group g, in order, and sums to 512.
All inputs are finite; a program needn't handle non-finite values.
Results may differ from a plain program's by a relative error of at most 0.009.
Values may be sent and summed in bfloat16 or wider, within the bound.
No kernel may reach another device: no remote copies, remote signals or barrier semaphores. Data moves between devices by JAX's collectives and lax.ppermute only.
A program may use at most 64 MiB of HBM per device.

v0:
```python
import math
import jax
import jax.numpy as jnp
from jax import lax
from jax.sharding import PartitionSpec as P

KVH = 8
HD = 128
PAGE = 32
REQS = 4
HITS = 4
CAPF = 6
CAPN = 2
EPSILON = 1e-06
ROPE_BASE = 1000000.0


def in_one_piece(arrays, axis, dim, along):
    ends, at = ([], 0)
    for a in arrays[:-1]:
        at += a.shape[along]
        ends.append(at)
    both = jnp.concatenate(arrays, axis=along)
    return tuple(jnp.split(lax.all_gather(both, axis, axis=dim, tiled=True), ends, axis=along))


def partner(value, axis, stride):
    mask = 2**stride
    pairs = [(source, source ^ mask) for source in range(lax.axis_size(axis))]
    return lax.ppermute(value, axis, pairs)


def rotate(values, positions):
    half = values.shape[-1] // 2
    steps_range = jnp.arange(half, dtype=jnp.float32)
    frequency = ROPE_BASE ** (-2.0 * steps_range / values.shape[-1])
    angles = positions.astype(jnp.float32)[:, None, None] * frequency[None, None, :]
    cosine = jnp.cos(angles)
    sine = jnp.sin(angles)
    first_half = values[..., :half]
    second_half = values[..., half:]
    return jnp.concatenate(
        [first_half * cosine - second_half * sine, second_half * cosine + first_half * sine],
        axis=-1,
    )


def slot_table(owners_row, capacity, seats):
    count_items = owners_row.shape[0]
    item_index = jnp.arange(count_items, dtype=jnp.int32)
    earlier_same = (owners_row[:, None] == owners_row[None, :]) & (
        item_index[None, :] < item_index[:, None]
    )
    slots = jnp.sum(earlier_same.astype(jnp.int32), axis=1)
    targets = owners_row * capacity + slots
    seat_index = jnp.arange(seats, dtype=jnp.int32)
    return targets[:, None] == seat_index[None, :]


def join_stack(held_new, held_cached, upper_half, other_new, other_cached):
    held_new = jnp.where(
        upper_half,
        jnp.concatenate([other_new, held_new], axis=0),
        jnp.concatenate([held_new, other_new], axis=0),
    )
    held_cached = jnp.where(
        upper_half,
        jnp.concatenate([other_cached, held_cached], axis=0),
        jnp.concatenate([held_cached, other_cached], axis=0),
    )
    return (held_new, held_cached)


def unstack_columns(held):
    return held.transpose(1, 0, 2).reshape(held.shape[1], held.shape[0] * held.shape[2])


def body(tokens, lengths, hit_pages, new_owner, w_query, w_keyval, w_out, pool_pages):
    rows_dev = tokens.shape[0]
    tp_count = lax.axis_size("tp")
    pool_count = lax.axis_size("pool")
    tp_rank = lax.axis_index("tp")
    group_rows = rows_dev * tp_count
    query_width = w_query.shape[1]
    part_width = w_keyval.shape[1] // 2
    heads_here = query_width // HD
    sharing = tp_count // KVH
    pages_here = pool_pages.shape[0]
    keyval_local = w_keyval.reshape(w_keyval.shape[0] * 2, part_width)
    pages_flat = pool_pages.reshape(pages_here, pool_pages.shape[1] * pool_pages.shape[2])
    tokens_wide = tokens.astype(jnp.float32)
    normed = (
        tokens_wide
        * lax.rsqrt(jnp.mean(tokens_wide * tokens_wide, axis=1, keepdims=True) + EPSILON)
    ).astype(jnp.bfloat16)
    full_query, full_keyval = in_one_piece((w_query, keyval_local), "pool", 0, 1)
    row_piece = lax.all_gather(normed, "tp", axis=0, tiled=True)
    projected = jnp.concatenate(
        [
            jnp.dot(row_piece, full_query, preferred_element_type=jnp.float32),
            jnp.dot(row_piece, full_keyval, preferred_element_type=jnp.float32),
        ],
        axis=1,
    )
    lengths_row = lengths[0]
    ends_at = jnp.cumsum(lengths_row)
    starts_at = ends_at - lengths_row
    token_index = jnp.arange(group_rows, dtype=jnp.int32)
    request_ids = jnp.sum((token_index[:, None] >= ends_at[None, :]).astype(jnp.int32), axis=1)
    chosen = request_ids[:, None] == jnp.arange(REQS, dtype=jnp.int32)[None, :]
    start_of = jnp.sum(jnp.where(chosen, starts_at[None, :], 0), axis=1)
    positions = token_index - start_of + HITS * PAGE
    queries = rotate(
        projected[:, :query_width].reshape(group_rows, heads_here, HD), positions
    ).astype(jnp.bfloat16)
    keyval_part = projected[:, query_width:].astype(jnp.bfloat16)
    page_ids = hit_pages.reshape(-1)
    count_hits = page_ids.shape[0]
    placed_hits = slot_table(page_ids // pages_here, CAPF, pool_count * CAPF)
    wanted = jnp.sum(jnp.where(placed_hits, (page_ids % pages_here)[:, None], 0), axis=0)
    wanted = wanted.reshape(pool_count, CAPF)
    asked = lax.all_to_all(wanted, "pool", split_axis=0, concat_axis=0, tiled=True)
    found = jnp.take(pages_flat, asked.reshape(-1), axis=0)
    found = found.reshape(asked.shape[0], asked.shape[1], pages_flat.shape[1])
    returned = lax.all_to_all(found, "pool", split_axis=0, concat_axis=0, tiled=True)
    returned = returned.reshape(pool_count * CAPF, PAGE * part_width)
    cached_part = jnp.dot(
        placed_hits.astype(jnp.bfloat16), returned, preferred_element_type=jnp.float32
    ).astype(jnp.bfloat16)
    cached_part = cached_part.reshape(count_hits * PAGE, part_width)
    bit_count = sharing.bit_length() - 1
    held_new = keyval_part[None]
    held_cached = cached_part[None]
    for bit_number in range(bit_count):
        other_new, other_cached = partner((held_new, held_cached), "tp", bit_number)
        upper_half = tp_rank // 2**bit_number % 2 == 1
        held_new, held_cached = join_stack(
            held_new, held_cached, upper_half, other_new, other_cached
        )
    new_head = unstack_columns(held_new)
    cached_head = unstack_columns(held_cached)
    new_keys = (
        rotate(new_head[:, :HD].astype(jnp.float32).reshape(group_rows, 1, HD), positions)
        .astype(jnp.bfloat16)
        .reshape(group_rows, HD)
    )
    stored_head = jnp.concatenate([new_keys, new_head[:, HD:]], axis=1)
    own_columns = lax.dynamic_slice_in_dim(
        stored_head, tp_rank % sharing * part_width, part_width, 1
    )
    page_count = group_rows // PAGE
    page_rows = own_columns.reshape(page_count, PAGE * part_width)
    placed_new = slot_table(new_owner[0], CAPN, pool_count * CAPN).astype(jnp.bfloat16)
    outgoing = jnp.dot(placed_new.T, page_rows, preferred_element_type=jnp.float32).astype(
        jnp.bfloat16
    )
    outgoing = outgoing.reshape(pool_count, CAPN, PAGE * part_width)
    new_store = lax.all_to_all(outgoing, "pool", split_axis=0, concat_axis=0, tiled=True).reshape(
        pool_count * CAPN, 1, PAGE * part_width
    )
    keys_all = jnp.concatenate([cached_head[:, :HD], new_keys], axis=0)
    values_all = jnp.concatenate([cached_head[:, HD:], new_head[:, HD:]], axis=0)
    cached_rows = count_hits * PAGE
    key_request = jnp.concatenate(
        [jnp.arange(cached_rows, dtype=jnp.int32) // (HITS * PAGE), request_ids]
    )
    key_order = jnp.concatenate([jnp.full((cached_rows,), -1, jnp.int32), token_index])
    block_rows = min(group_rows, 512)

    def attend(first_row):
        scores = jnp.einsum(
            "bhd,kd->hbk", queries, keys_all, preferred_element_type=jnp.float32
        ) / math.sqrt(HD)
        visible = (request_ids[:, None] == key_request[None, :]) & (
            key_order[None, :] <= token_index[:, None]
        )
        scores = jnp.where(visible[None], scores, -jnp.inf)
        highest = jnp.max(scores, axis=-1, keepdims=True)
        expanded = jnp.exp(scores - highest)
        weights = (expanded / jnp.sum(expanded, axis=-1, keepdims=True)).astype(jnp.bfloat16)
        blended = jnp.einsum(
            "hbk,kd->bhd", weights, values_all, preferred_element_type=jnp.float32
        ).astype(jnp.bfloat16)
        return blended.reshape(block_rows, query_width)

    attended = lax.map(
        attend, jnp.arange(group_rows // block_rows, dtype=jnp.int32) * block_rows
    ).reshape(group_rows, query_width)
    full_out = lax.all_gather(w_out, "pool", axis=1, tiled=True)
    summed = lax.psum_scatter(
        jnp.dot(attended, full_out, preferred_element_type=jnp.float32).astype(jnp.bfloat16),
        "tp",
        scatter_dimension=0,
        tiled=True,
    ).astype(jnp.float32)
    mixed = tokens_wide + summed
    return (mixed, new_store)


def solution(mesh):
    return jax.shard_map(
        body,
        mesh=mesh,
        in_specs=(
            P(("pool", "tp"), None),
            P("pool", None),
            P("pool", None, None),
            P("pool", None),
            P("pool", "tp"),
            P("pool", "tp"),
            P("tp", "pool"),
            P("pool", "tp", None),
        ),
        out_specs=(P(("pool", "tp"), None), P("pool", "tp", None)),
        check_vma=False,
    )
```

profile of v0, /device:TPU:2, one launch (start us, length us, event | category | flops | bytes accessed | tf_op | source)
XLA Modules:
  0.0 323.8 jit_solution(13723968068413563517)
XLA Ops:
  7.3 1.2 reshape.404
  8.4 2.0 pad_maximum_fusion
  10.6 1.1 fusion.18
  11.7 1.8 fusion.19
  13.6 0.7 all-gather.8.cloned.1.call-update
  14.4 0.2 convert_reduce_fusion.2
  14.6 0.7 all_to_all.12
  15.3 8.5 %all-to-all-start = ((s32[8,1,6]{2,1,0:T(1,128)}), s32[8,1,6]{2,1,0:T(1,128)S(1)}, u32[]{:S(2)}, u32[]{:S(2)}) async-start(s32[8,1,6]{2,1,0:T(1,128)} %bitcast), calls=%async_computation | async-start | bytes 8192 | tf_op jit(solution)/shard_map/all_to_all | solution.py:122
  23.8 0.2 reduce-window.4
  24.2 7.4 %all-to-all-done = s32[8,1,6]{2,1,0:T(1,128)S(1)} async-done(((s32[8,1,6]{2,1,0:T(1,128)}), s32[8,1,6]{2,1,0:T(1,128)S(1)}, u32[]{:S(2)}, u32[]{:S(2)}) %all-to-all-start) | async-done | bytes 224 | tf_op jit(solution)/shard_map/all_to_all | solution.py:122
  31.5 0.5 broadcast.349
  32.0 0.7 reduce.3
  32.8 0.7 gather_fusion
  33.6 0.8 broadcast_select_fusion
  34.4 3.4 %all-to-all-start.1 = ((bf16[8,6,2048]{2,1,0:T(8,128)(2,1)}), bf16[8,6,2048]{2,1,0:T(8,128)(2,1)S(1)}, u32[]{:S(2)}, u32[]{:S(2)}) async-start(bf16[8,6,2048]{2,1,0:T(8,128)(2,1)} %broadcast_select_fusion), calls=%async_computation.1 | async-start | bytes 524288 | tf_op jit(solution)/shard_map/all_to_all | solution.py:125
  37.9 1.5 fusion.8
  39.4 13.0 %all-to-all-done.1 = bf16[8,6,2048]{2,1,0:T(8,128)(2,1)S(1)} async-done(((bf16[8,6,2048]{2,1,0:T(8,128)(2,1)}), bf16[8,6,2048]{2,1,0:T(8,128)(2,1)S(1)}, u32[]{:S(2)}, u32[]{:S(2)}) %all-to-all-start.1) | async-done | bytes 196640 | tf_op jit(solution)/shard_map/all_to_all | solution.py:125
  52.5 0.2 convolution_convert_fusion.2
  52.7 0.2 broadcast_in_dim_reshape.3
  53.1 1.2 collective-permute-done
  54.3 1.7 collective-permute-start.1
  56.0 1.8 multiply_cosine_fusion
  57.8 2.2 collective-permute-done.1
  60.0 0.7 maximum_select_fusion
  60.7 33.0 %all-gather.6.cloned.1.call-done = bf16[8192,320]{1,0:T(8,128)(2,1)} async-done(((bf16[1024,320]{1,0:T(8,128)(2,1)}), bf16[8192,320]{1,0:T(8,128)(2,1)}) %all-gather.6.cloned.1.call-update) | async-done | bytes 5242896 | tf_op jit(solution)/shard_map/all_gather | solution.py:24
  93.7 59.0 %all-gather.4.cloned.1.call-done = bf16[512,8192]{1,0:T(8,128)(2,1)} async-done(((bf16[16,8192]{1,0:T(8,128)(2,1)}), bf16[512,8192]{1,0:T(8,128)(2,1)}) %all-gather.4.cloned.1.call-update) | async-done | bytes 8388624 | tf_op jit(solution)/shard_map/all_gather | solution.py:97
  152.7 6.8 %fusion.15 = bf16[1,512,64]{1,2,0:T(8,128)(2,1)S(1)} fusion(bf16[512,8192]{1,0:T(8,128)(2,1)} %all-gather.4.cloned.1.call-done, bf16[8192,320]{1,0:T(8,128)(2,1)} %all-gather.6.cloned.1.call-done), kind=kOutput, calls=%fused_computation.21 | convolution fusion | flops 536903680 | bytes 10551296 | tf_op jit(solution)/shard_map/dot_general | solution.py:101
  159.4 0.3 collective-permute-start.2
  159.8 4.6 %fusion.1 = f32[512,256]{0,1:T(8,128)S(1)} fusion(bf16[512,8192]{1,0:T(8,128)(2,1)S(1)} %copy-done.1, bf16[8192,320]{1,0:T(8,128)(2,1)} %all-gather.6.cloned.1.call-done), kind=kOutput, calls=%fused_computation.3 | convolution fusion | flops 2147483648 | bytes 13107200 | tf_op jit(solution)/shard_map/dot_general | solution.py:100
  164.4 0.2 copy.58
  164.7 0.2 copy.59
  164.9 0.4 collective-permute-start.3
  165.3 1.9 subtract_convert_fusion
  167.2 3.6 %collective-permute-done.3 = bf16[2,512,64]{1,2,0:T(8,128)(2,1)S(1)} collective-permute-done((bf16[2,512,64]{1,2,0:T(8,128)(2,1)S(1)}, bf16[2,512,64]{1,2,0:T(8,128)(2,1)S(1)}, u32[]{:S(2)}, u32[]{:S(2)}) %collective-permute-start.3) | collective-permute-done | bytes 131104 | tf_op jit(solution)/shard_map/ppermute | solution.py:30
  170.9 1.0 fusion.54
  172.1 1.2 fusion.33
  173.4 4.8 %fusion.56 = (f32[2,512]{1,0:T(2,128)S(1)}, f32[2,512,1024]{1,2,0:T(8,128)}) fusion(pred[512,1024]{0,1:T(8,128)(4,1)} %fusion.8, bf16[512,64]{1,0:T(8,128)(2,1)S(1)} %get-tuple-element.25, bf16[512,64]{1,0:T(8,128)(2,1)S(1)} %get-tuple-element.24, bf16[512,128]{1,0:T(8,128)(2,1)S(1)} %copy.56, bf16[512,2,64]{2,0,1:T(8,128)(2,1)} %get-tuple-element.21, ...), kind=kOutput, calls=%fused_computation.109 | convolution fusion | flops 273941504 | bytes 5246976 | tf_op jit(solution)/shard_map/while/body/eval_jaxpr/sub | solution.py:179
  178.2 2.7 fusion.11
  180.8 28.1 %all-gather.8.cloned.1.call-done = bf16[256,8192]{1,0:T(8,128)(2,1)} async-done(((bf16[256,1024]{1,0:T(8,128)(2,1)}), bf16[256,8192]{1,0:T(8,128)(2,1)}) %all-gather.8.cloned.1.call-update) | async-done | bytes 4194320 | tf_op jit(solution)/shard_map/all_gather | solution.py:189
  208.9 7.8 %convolution_convert_fusion = bf16[512,8192]{1,0:T(8,128)(2,1)} fusion(bf16[512,256]{0,1:T(8,128)(2,1)S(1)} %bitcast.70, bf16[256,8192]{1,0:T(8,128)(2,1)} %all-gather.8.cloned.1.call-done), kind=kOutput, calls=%fused_computation.2 | convolution fusion | flops 2151677952 | bytes 12845056 | tf_op jit(solution)/shard_map/dot_general | solution.py:191
  216.7 0.6 copy-done.6
  217.3 0.2 convert_reduce_fusion
  218.0 0.2 reshape.412
  218.2 0.3 convolution_convert_fusion.1
  218.5 12.5 %all_to_all.19 = bf16[8,2,2048]{2,1,0:T(2,128)(2,1)S(1)} all-to-all(bf16[8,2,2048]{2,1,0:T(2,128)(2,1)S(1)} %reshape.413), channel_id=1, replica_groups=mesh['pool'=8,'tp'=32] {'pool'}, dimensions={0} | all-to-all | bytes 131072 | tf_op jit(solution)/shard_map/all_to_all | solution.py:158
  231.0 0.7 reshape.414
  231.7 83.8 %reduce-scatter.2.cloned.1.call-done = bf16[16,8192]{1,0:T(8,128)(2,1)} async-done(((bf16[512,8192]{1,0:T(8,128)(2,1)}), bf16[16,8192]{1,0:T(8,128)(2,1)}) %reduce-scatter.2.cloned.1.call-update) | async-done | bytes 262160 | tf_op jit(solution)/shard_map/reduce_scatter | solution.py:190
  315.5 1.8 convert_add_fusion
  (54 shorter events, 1.9 us)
Async XLA Ops:
  7.2 25.6 %copy-start = (bf16[512,1,2048]{2,0,1:T(8,128)(2,1)S(1)}, bf16[512,1,2048]{2,0,1:T(8,128)(2,1)}, u32[]{:S(2)}) copy-start(bf16[512,1,2048]{2,0,1:T(8,128)(2,1)} %param.15) | copy-start | bytes 6291460
  7.2 30.7 %copy-start.3 = (s32[1024]{0:T(1024)S(1)}, s32[1024]{0:T(1024)}, u32[]{:S(2)}) copy-start(s32[1024]{0:T(1024)} %constant.140.clone.1) | copy-start | bytes 12292
  7.2 7.1 %copy-start.4 = (s32[1,4,4]{2,1,0:T(4,128)S(1)}, s32[1,4,4]{2,1,0:T(4,128)}, u32[]{:S(2)}) copy-start(s32[1,4,4]{2,1,0:T(4,128)} %param.10) | copy-start | bytes 196
  7.2 16.6 %copy-start.5 = (s32[1,4]{1,0:T(1,128)S(1)}, s32[1,4]{1,0:T(1,128)}, u32[]{:S(2)}) copy-start(s32[1,4]{1,0:T(1,128)} %param.9) | copy-start | bytes 52
  7.2 86.5 %all-gather.6.cloned.1.call-start = ((), (), s32[]{:S(2)}) async-start(), calls=%async_computation.5 | async-start | bytes 7077888 | tf_op jit(solution)/shard_map/all_gather | solution.py:24
  10.5 142.2 %all-gather.4.cloned.1.call-start = ((), (), s32[]{:S(2)}) async-start(), calls=%async_computation.4 | async-start | bytes 8650752 | tf_op jit(solution)/shard_map/all_gather | solution.py:97
  13.5 195.4 %all-gather.8.cloned.1.call-start = ((), (), s32[]{:S(2)}) async-start(), calls=%async_computation.6 | async-start | bytes 4718592 | tf_op jit(solution)/shard_map/all_gather | solution.py:189
  15.3 16.2 %all-to-all-start = ((s32[8,1,6]{2,1,0:T(1,128)}), s32[8,1,6]{2,1,0:T(1,128)S(1)}, u32[]{:S(2)}, u32[]{:S(2)}) async-start(s32[8,1,6]{2,1,0:T(1,128)} %bitcast), calls=%async_computation | async-start | bytes 8192 | tf_op jit(solution)/shard_map/all_to_all | solution.py:122
  34.4 18.0 %all-to-all-start.1 = ((bf16[8,6,2048]{2,1,0:T(8,128)(2,1)}), bf16[8,6,2048]{2,1,0:T(8,128)(2,1)S(1)}, u32[]{:S(2)}, u32[]{:S(2)}) async-start(bf16[8,6,2048]{2,1,0:T(8,128)(2,1)} %broadcast_select_fusion), calls=%async_computation.1 | async-start | bytes 524288 | tf_op jit(solution)/shard_map/all_to_all | solution.py:125
  37.8 277.7 %reduce-scatter.2.cloned.1.call-start = ((), (), s32[]{:S(2)}) async-start(), calls=%async_computation.7 | async-start | bytes 8650752 | tf_op jit(solution)/shard_map/reduce_scatter | solution.py:190
  53.0 1.3 collective-permute-start
  54.3 5.6 %collective-permute-start.1 = (bf16[2,512,64]{1,2,0:T(8,128)(2,1)S(1)}, bf16[2,512,64]{1,2,0:T(8,128)(2,1)S(1)}, u32[]{:S(2)}, u32[]{:S(2)}) collective-permute-start(bf16[2,512,64]{1,2,0:T(8,128)(2,1)S(1)} %maximum_select_fusion.2), channel_id=1, source_target_pairs={{0,2},{1,3},{2,0},{3,1},{4,6},{5,7},{6,4},{7,5},{8,10},{9,11},{10,... | collective-permute-start | bytes 393224 | tf_op jit(solution)/shard_map/ppermute | solution.py:30
  152.7 7.1 %copy-start.1 = (bf16[512,8192]{1,0:T(8,128)(2,1)S(1)}, bf16[512,8192]{1,0:T(8,128)(2,1)}, u32[]{:S(2)}) copy-start(bf16[512,8192]{1,0:T(8,128)(2,1)} %all-gather.4.cloned.1.call-done) | copy-start | bytes 25165828
  159.4 5.4 %collective-permute-start.2 = (bf16[1,512,64]{1,2,0:T(8,128)(2,1)S(1)}, bf16[1,512,64]{1,2,0:T(8,128)(2,1)S(1)}, u32[]{:S(2)}, u32[]{:S(2)}) collective-permute-start(bf16[1,512,64]{1,2,0:T(8,128)(2,1)S(1)} %fusion.15), channel_id=1, source_target_pairs={{0,1},{1,0},{2,3},{3,2},{4,5},{5,4},{6,7},{7,6},{8,9},{9,8},{10,11... | collective-permute-start | bytes 196616 | tf_op jit(solution)/shard_map/ppermute | solution.py:30
  164.9 5.9 %collective-permute-start.3 = (bf16[2,512,64]{1,2,0:T(8,128)(2,1)S(1)}, bf16[2,512,64]{1,2,0:T(8,128)(2,1)S(1)}, u32[]{:S(2)}, u32[]{:S(2)}) collective-permute-start(bf16[2,512,64]{1,2,0:T(8,128)(2,1)S(1)} %maximum_select_fusion.3), channel_id=1, source_target_pairs={{0,2},{1,3},{2,0},{3,1},{4,6},{5,7},{6,4},{7,5},{8,10},{9,11},{10,... | collective-permute-start | bytes 393224 | tf_op jit(solution)/shard_map/ppermute | solution.py:30
  216.7 0.7 copy-start.6
  216.7 98.8 %copy-start.2 = (bf16[16,8192]{1,0:T(8,128)(2,1)S(1)}, bf16[16,8192]{1,0:T(8,128)(2,1)}, u32[]{:S(2)}) copy-start(bf16[16,8192]{1,0:T(8,128)(2,1)} %param.8) | copy-start | bytes 786436
Sparse Core Ops, SparseCore 0:
  10.6 83.0 all-gather.5
  96.2 56.3 all-gather.3
  154.5 54.4 all-gather.7
  216.8 98.6 reduce-scatter.1
where the time goes:
time: 324 us
  waiting for transfers between devices  232 us (72%)
  matrix products  27.1 us (8%)
  other arithmetic  16.5 us (5%)
  starting transfers between devices  14.5 us (4%)
  between operations  14.1 us (4%)
  blocking collectives  12.5 us (4%)
  local copies, waits for them, and re-layouts  7.18 us (2%)
    reduce_scatter x1, waiting for transfers between devices, body(): lax.psum_scatter(jnp.dot(attended, full_out, preferred_element_type=jnp.f...  83.8 us
    all_gather x1, waiting for transfers between devices, body(): row_piece = lax.all_gather(normed, 'tp', axis=0, tiled=True)  59 us
    all_gather x1, waiting for transfers between devices, in_one_piece(): lax.all_gather(both, axis, axis=dim, tiled=True)  33 us
    all_gather x1, waiting for transfers between devices, body(): full_out = lax.all_gather(w_out, 'pool', axis=1, tiled=True)  28.1 us
    all_to_all x1, waiting for transfers between devices, body(): lax.all_to_all(found, 'pool', split_axis=0, concat_axis=0, tiled=True)  13 us
    all_to_all x1, blocking collectives, body(): lax.all_to_all(outgoing, 'pool', split_axis=0, concat_axis=0, tiled=True)  12.5 us
    all_to_all x1, starting transfers between devices, body(): lax.all_to_all(wanted, 'pool', split_axis=0, concat_axis=0, tiled=True)  8.47 us
    dot_general x1, matrix products, body(): jnp.dot(attended, full_out, preferred_element_type=jnp.float32)  7.77 us
  transfers between devices with their start and end apart: 10, of which 9 were waited for; matrix products, arithmetic and copies ran while one was open for 11% of the time, Pallas kernels for 0%

commit v1 on v0

--- a/solution.py
+++ b/solution.py
@@ -94,7 +94,8 @@
         * lax.rsqrt(jnp.mean(tokens_wide * tokens_wide, axis=1, keepdims=True) + EPSILON)
     ).astype(jnp.bfloat16)
     full_query, full_keyval = in_one_piece((w_query, keyval_local), "pool", 0, 1)
-    row_piece = lax.all_gather(normed, "tp", axis=0, tiled=True)
+    copies = jnp.concatenate([normed] * lax.axis_size("tp"), axis=0)
+    row_piece = lax.all_to_all(copies, "tp", 0, 0, tiled=True)
     projected = jnp.concatenate(
         [
             jnp.dot(row_piece, full_query, preferred_element_type=jnp.float32),

time: 324 us -> 363 us (1.12)
  other arithmetic: 16.5 us -> 46.6 us
  waiting for transfers between devices: 232 us -> 207 us
  starting transfers between devices: 14.5 us -> 37.8 us
  local copies, waits for them, and re-layouts: 7.18 us -> 16.7 us
    ppermute x4, waiting for transfers between devices: 7.03 us -> 95.4 us  [partner(): return lax.ppermute(value, axis, pairs)]
    all_gather x1 -> x0, waiting for transfers between devices: 59 us -> none  [body(): row_piece = lax.all_gather(normed, 'tp', axis=0, tiled=True)]
    unnamed x0 -> x31, other arithmetic: none -> 34.9 us
    all_gather x1, waiting for transfers between devices: 33 us -> 0.01 us  [in_one_piece(): lax.all_gather(both, axis, axis=dim, tiled=True)]
    all_gather x1, waiting for transfers between devices: 28.1 us -> 0.02 us  [body(): full_out = lax.all_gather(w_out, 'pool', axis=1, tiled=True)]
    ppermute x4, starting transfers between devices: 2.5 us -> 14.2 us  [partner(): return lax.ppermute(value, axis, pairs)]
    dot_general x0 -> x2, local copies, waits for them, and re-layouts: none -> 8.57 us  [body(): jnp.dot(row_piece, full_query, preferred_element_type=jnp.float32)]
    all_to_all x0 -> x1, starting transfers between devices: none -> 7.81 us  [body(): row_piece = lax.all_to_all(copies, 'tp', 0, 0, tiled=True)]
  transfers between devices with their start and end apart: 10 -> 10, of which waited for: 9 -> 6; matrix products, arithmetic and copies ran while one was open for 11% -> 22% of each run, Pallas kernels for 0% -> 0%
where the time goes in v1:
time: 363 us; the launch traced here: 362 us
  waiting for transfers between devices  207 us (57%)
  other arithmetic  46.6 us (13%)
  starting transfers between devices  37.8 us (10%)
  matrix products  29.2 us (8%)
  local copies, waits for them, and re-layouts  16.7 us (5%)
  between operations  14.1 us (4%)
  blocking collectives  10.8 us (3%)
    ppermute x4, waiting for transfers between devices, partner(): return lax.ppermute(value, axis, pairs)  95.4 us
    reduce_scatter x1, waiting for transfers between devices, body(): lax.psum_scatter(jnp.dot(attended, full_out, preferred_element_type=jnp.f...  89.7 us
    unnamed x31, other arithmetic  34.9 us
    ppermute x4, starting transfers between devices, partner(): return lax.ppermute(value, axis, pairs)  14.2 us
    all_to_all x1, waiting for transfers between devices, body(): lax.all_to_all(found, 'pool', split_axis=0, concat_axis=0, tiled=True)  14.2 us
    all_to_all x1, blocking collectives, body(): lax.all_to_all(outgoing, 'pool', split_axis=0, concat_axis=0, tiled=True)  10.8 us
    dot_general x2, local copies, waits for them, and re-layouts, body(): jnp.dot(row_piece, full_query, preferred_element_type=jnp.float32)  8.57 us
    all_to_all x1, starting transfers between devices, body(): lax.all_to_all(wanted, 'pool', split_axis=0, concat_axis=0, tiled=True)  8.47 us
  transfers between devices with their start and end apart: 10, of which 6 were waited for; matrix products, arithmetic and copies ran while one was open for 22% of the time, Pallas kernels for 0%

profile of v1, /device:TPU:2, one launch (start us, length us, event | category | flops | bytes accessed | tf_op | source)
XLA Modules:
  0.0 362.4 jit_solution(9961857199882304384)
XLA Ops:
  7.2 1.2 reshape.405
  8.5 2.0 pad_maximum_fusion
  12.2 8.5 %all-to-all-start = ((s32[8,1,6]{2,1,0:T(1,128)}), s32[8,1,6]{2,1,0:T(1,128)S(1)}, u32[]{:S(2)}, u32[]{:S(2)}) async-start(s32[8,1,6]{2,1,0:T(1,128)} %bitcast), calls=%async_computation | async-start | bytes 8192 | tf_op jit(solution)/shard_map/all_to_all | solution.py:123
  20.7 1.1 fusion.16
  21.8 1.8 constant_dynamic-update-slice_fusion.31
  23.6 1.8 constant_dynamic-update-slice_fusion.30
  25.4 1.8 constant_dynamic-update-slice_fusion.29
  27.2 1.8 constant_dynamic-update-slice_fusion.28
  28.9 1.8 constant_dynamic-update-slice_fusion.27
  30.7 1.8 constant_dynamic-update-slice_fusion.26
  32.5 1.8 constant_dynamic-update-slice_fusion.25
  34.3 1.8 constant_dynamic-update-slice_fusion.24
  36.0 1.8 constant_dynamic-update-slice_fusion.23
  37.8 1.8 constant_dynamic-update-slice_fusion.22
  39.6 0.8 constant_dynamic-update-slice_fusion.21
  43.7 0.8 constant_dynamic-update-slice_fusion.16
  44.5 0.8 constant_dynamic-update-slice_fusion.15
  45.3 0.8 constant_dynamic-update-slice_fusion.14
  46.2 0.8 constant_dynamic-update-slice_fusion.13
  47.0 0.8 constant_dynamic-update-slice_fusion.12
  50.2 0.8 constant_dynamic-update-slice_fusion.8
  51.0 0.8 constant_dynamic-update-slice_fusion.7
  51.9 0.8 constant_dynamic-update-slice_fusion.6
  52.7 0.8 constant_dynamic-update-slice_fusion.5
  55.1 0.8 constant_dynamic-update-slice_fusion.2
  59.7 7.2 %all-to-all-start.1 = ((bf16[8,6,2048]{2,1,0:T(8,128)(2,1)}), bf16[8,6,2048]{2,1,0:T(8,128)(2,1)S(1)}, u32[]{:S(2)}, u32[]{:S(2)}) async-start(bf16[8,6,2048]{2,1,0:T(8,128)(2,1)} %broadcast_select_fusion), calls=%async_computation.1 | async-start | bytes 524288 | tf_op jit(solution)/shard_map/all_to_all | solution.py:126
  66.9 0.8 constant_dynamic-update-slice_fusion
  67.7 14.2 %all-to-all-done.1 = bf16[8,6,2048]{2,1,0:T(8,128)(2,1)S(1)} async-done(((bf16[8,6,2048]{2,1,0:T(8,128)(2,1)}), bf16[8,6,2048]{2,1,0:T(8,128)(2,1)S(1)}, u32[]{:S(2)}, u32[]{:S(2)}) %all-to-all-start.1) | async-done | bytes 196640 | tf_op jit(solution)/shard_map/all_to_all | solution.py:126
  81.9 7.8 %all-to-all-start.2 = ((bf16[32,16,8192]{2,1,0:T(8,128)(2,1)}), bf16[32,16,8192]{2,1,0:T(8,128)(2,1)}, u32[]{:S(2)}, u32[]{:S(2)}) async-start(bf16[32,16,8192]{2,1,0:T(8,128)(2,1)} %bitcast.6), calls=%async_computation.2 | async-start | bytes 16777216 | tf_op jit(solution)/shard_map/all_to_all | solution.py:98
  90.9 0.8 fusion.6
  92.6 1.1 collective-permute-done
  93.7 1.6 collective-permute-start.1
  95.8 91.3 %collective-permute-done.1 = bf16[2,512,64]{1,2,0:T(8,128)(2,1)S(1)} collective-permute-done((bf16[2,512,64]{1,2,0:T(8,128)(2,1)S(1)}, bf16[2,512,64]{1,2,0:T(8,128)(2,1)S(1)}, u32[]{:S(2)}, u32[]{:S(2)}) %collective-permute-start.1) | collective-permute-done | bytes 131104 | tf_op jit(solution)/shard_map/ppermute | solution.py:30
  187.2 7.1 %all-to-all-done.2 = bf16[32,16,8192]{2,1,0:T(8,128)(2,1)} async-done(((bf16[32,16,8192]{2,1,0:T(8,128)(2,1)}), bf16[32,16,8192]{2,1,0:T(8,128)(2,1)}, u32[]{:S(2)}, u32[]{:S(2)}) %all-to-all-start.2) | async-done | bytes 8388640 | tf_op jit(solution)/shard_map/all_to_all | solution.py:98
  194.3 6.8 %fusion.13 = bf16[1,512,64]{1,2,0:T(8,128)(2,1)S(1)} fusion(bf16[512,8192]{1,0:T(8,128)(2,1)} %bitcast.7, bf16[8192,320]{1,0:T(8,128)(2,1)} %all-gather.3.cloned.1.call-done), kind=kOutput, calls=%fused_computation.20 | convolution fusion | flops 536903680 | bytes 10551296 | tf_op jit(solution)/shard_map/dot_general | solution.py:102
  201.4 2.2 slice_bitcast_fusion
  203.7 6.3 %copy.49 = bf16[256,8192]{1,0:T(8,128)(2,1)} copy(bf16[256,8192]{0,1:T(8,128)(2,1)} %slice_bitcast_fusion) | data formatting | bytes 8388608 | tf_op jit(solution)/shard_map/dot_general | solution.py:101
  210.0 6.9 %fusion.54 = f32[512,2,128]{0,2,1:T(8,128)S(1)} fusion(bf16[512,8192,1]{1,0,2:T(8,128)(2,1)} %bitcast.23, bf16[2,128,8192]{2,1,0:T(8,128)(2,1)} %bitcast.72), kind=kOutput, calls=%fused_computation.140 | convolution fusion | flops 2147483648 | bytes 13107200 | tf_op jit(solution)/shard_map/dot_general | solution.py:101
  217.0 12.2 %collective-permute-start.3 = (bf16[2,512,64]{1,2,0:T(8,128)(2,1)S(1)}, bf16[2,512,64]{1,2,0:T(8,128)(2,1)S(1)}, u32[]{:S(2)}, u32[]{:S(2)}) collective-permute-start(bf16[2,512,64]{1,2,0:T(8,128)(2,1)S(1)} %maximum_select_fusion.3), channel_id=1, source_target_pairs={{0,2},{1,3},{2,0},{3,1},{4,6},{5,7},{6,4},{7,5},{8,10},{9,11},{10,... | collective-permute-start | bytes 393224 | tf_op jit(solution)/shard_map/ppermute | solution.py:30
  230.0 2.9 collective-permute-done.3
  233.6 1.0 copy.58
  235.4 1.2 fusion.32
  236.7 4.6 %fusion.53 = (f32[2,512]{1,0:T(2,128)S(1)}, f32[2,512,1024]{1,2,0:T(8,128)}) fusion(pred[512,1024]{0,1:T(8,128)(4,1)S(1)} %fusion.6, bf16[512,2,64]{0,2,1:T(8,128)(2,1)} %get-tuple-element.21, bf16[512,2,64]{0,2,1:T(8,128)(2,1)} %get-tuple-element.20, bf16[512,64]{1,0:T(8,128)(2,1)S(1)} %get-tuple-element.23, bf16[512,64]{1,0:T(8,128)(2,1)S(1)} %get-tuple-element.22, ...), kind=kOutput, calls=%fused_computation.139 | convolution fusion | flops 273941504 | bytes 5246976 | tf_op jit(solution)/shard_map/while/body/eval_jaxpr/sub | solution.py:180
  241.3 2.6 fusion.9
  244.0 7.8 %convolution_convert_fusion = bf16[512,8192]{1,0:T(8,128)(2,1)} fusion(bf16[512,256]{0,1:T(8,128)(2,1)S(1)} %bitcast.75, bf16[256,8192]{1,0:T(8,128)(2,1)} %all-gather.5.cloned.1.call-done), kind=kOutput, calls=%fused_computation.2 | convolution fusion | flops 2151677952 | bytes 12845056 | tf_op jit(solution)/shard_map/dot_general | solution.py:192
  253.0 10.8 %all_to_all.31 = bf16[8,2,2048]{2,1,0:T(2,128)(2,1)S(1)} all-to-all(bf16[8,2,2048]{2,1,0:T(2,128)(2,1)S(1)} %reshape.413), channel_id=1, replica_groups=mesh['pool'=8,'tp'=32] {'pool'}, dimensions={0} | all-to-all | bytes 131072 | tf_op jit(solution)/shard_map/all_to_all | solution.py:159
  264.4 89.7 %reduce-scatter.2.cloned.1.call-done = bf16[16,8192]{1,0:T(8,128)(2,1)} async-done(((bf16[512,8192]{1,0:T(8,128)(2,1)}), bf16[16,8192]{1,0:T(8,128)(2,1)}) %reduce-scatter.2.cloned.1.call-update) | async-done | bytes 262160 | tf_op jit(solution)/shard_map/reduce_scatter | solution.py:191
  354.1 1.8 convert_add_fusion
  (83 shorter events, 19.7 us)
Async XLA Ops:
  7.2 50.9 %copy-start = (bf16[512,1,2048]{2,0,1:T(8,128)(2,1)S(1)}, bf16[512,1,2048]{2,0,1:T(8,128)(2,1)}, u32[]{:S(2)}) copy-start(bf16[512,1,2048]{2,0,1:T(8,128)(2,1)} %param.15) | copy-start | bytes 6291460
  7.2 32.4 %copy-start.1 = (bf16[16,8192]{1,0:T(8,128)(2,1)S(1)}, bf16[16,8192]{1,0:T(8,128)(2,1)}, u32[]{:S(2)}) copy-start(bf16[16,8192]{1,0:T(8,128)(2,1)} %param.8) | copy-start | bytes 786436
  7.2 187.2 %all-gather.3.cloned.1.call-start = ((), (), s32[]{:S(2)}) async-start(), calls=%async_computation.5 | async-start | bytes 7077888 | tf_op jit(solution)/shard_map/all_gather | solution.py:24
  12.2 44.6 %all-to-all-start = ((s32[8,1,6]{2,1,0:T(1,128)}), s32[8,1,6]{2,1,0:T(1,128)S(1)}, u32[]{:S(2)}, u32[]{:S(2)}) async-start(s32[8,1,6]{2,1,0:T(1,128)} %bitcast), calls=%async_computation | async-start | bytes 8192 | tf_op jit(solution)/shard_map/all_to_all | solution.py:123
  59.7 22.2 %all-to-all-start.1 = ((bf16[8,6,2048]{2,1,0:T(8,128)(2,1)}), bf16[8,6,2048]{2,1,0:T(8,128)(2,1)S(1)}, u32[]{:S(2)}, u32[]{:S(2)}) async-start(bf16[8,6,2048]{2,1,0:T(8,128)(2,1)} %broadcast_select_fusion), calls=%async_computation.1 | async-start | bytes 524288 | tf_op jit(solution)/shard_map/all_to_all | solution.py:126
  81.9 8.6 %copy-start.5 = (s32[1,4]{1,0:T(1,128)S(1)}, s32[1,4]{1,0:T(1,128)}, u32[]{:S(2)}) copy-start(s32[1,4]{1,0:T(1,128)} %param.9) | copy-start | bytes 52
  81.9 9.0 %copy-start.4 = (s32[1024]{0:T(1024)S(1)}, s32[1024]{0:T(1024)}, u32[]{:S(2)}) copy-start(s32[1024]{0:T(1024)} %constant.140.clone.1) | copy-start | bytes 12292
  81.9 112.4 %all-to-all-start.2 = ((bf16[32,16,8192]{2,1,0:T(8,128)(2,1)}), bf16[32,16,8192]{2,1,0:T(8,128)(2,1)}, u32[]{:S(2)}, u32[]{:S(2)}) async-start(bf16[32,16,8192]{2,1,0:T(8,128)(2,1)} %bitcast.6), calls=%async_computation.2 | async-start | bytes 16777216 | tf_op jit(solution)/shard_map/all_to_all | solution.py:98
  89.7 154.2 %all-gather.5.cloned.1.call-start = ((), (), s32[]{:S(2)}) async-start(), calls=%async_computation.6 | async-start | bytes 4718592 | tf_op jit(solution)/shard_map/all_gather | solution.py:190
  90.5 263.6 %reduce-scatter.2.cloned.1.call-start = ((), (), s32[]{:S(2)}) async-start(), calls=%async_computation.7 | async-start | bytes 8650752 | tf_op jit(solution)/shard_map/reduce_scatter | solution.py:191
  92.4 1.3 collective-permute-start
  93.7 93.4 %collective-permute-start.1 = (bf16[2,512,64]{1,2,0:T(8,128)(2,1)S(1)}, bf16[2,512,64]{1,2,0:T(8,128)(2,1)S(1)}, u32[]{:S(2)}, u32[]{:S(2)}) collective-permute-start(bf16[2,512,64]{1,2,0:T(8,128)(2,1)S(1)} %maximum_select_fusion.2), channel_id=1, source_target_pairs={{0,2},{1,3},{2,0},{3,1},{4,6},{5,7},{6,4},{7,5},{8,10},{9,11},{10,... | collective-permute-start | bytes 393224 | tf_op jit(solution)/shard_map/ppermute | solution.py:30
  194.3 7.1 %copy-start.2 = (bf16[8192,320]{1,0:T(8,128)(2,1)S(1)}, bf16[8192,320]{1,0:T(8,128)(2,1)}, u32[]{:S(2)}) copy-start(bf16[8192,320]{1,0:T(8,128)(2,1)} %all-gather.3.cloned.1.call-done) | copy-start | bytes 15728644
  201.1 15.8 %collective-permute-start.2 = (bf16[1,512,64]{1,2,0:T(8,128)(2,1)S(1)}, bf16[1,512,64]{1,2,0:T(8,128)(2,1)S(1)}, u32[]{:S(2)}, u32[]{:S(2)}) collective-permute-start(bf16[1,512,64]{1,2,0:T(8,128)(2,1)S(1)} %fusion.13), channel_id=1, source_target_pairs={{0,1},{1,0},{2,3},{3,2},{4,5},{5,4},{6,7},{7,6},{8,9},{9,8},{10,11... | collective-permute-start | bytes 196616 | tf_op jit(solution)/shard_map/ppermute | solution.py:30
  217.0 15.9 %collective-permute-start.3 = (bf16[2,512,64]{1,2,0:T(8,128)(2,1)S(1)}, bf16[2,512,64]{1,2,0:T(8,128)(2,1)S(1)}, u32[]{:S(2)}, u32[]{:S(2)}) collective-permute-start(bf16[2,512,64]{1,2,0:T(8,128)(2,1)S(1)} %maximum_select_fusion.3), channel_id=1, source_target_pairs={{0,2},{1,3},{2,0},{3,1},{4,6},{5,7},{6,4},{7,5},{8,10},{9,11},{10,... | collective-permute-start | bytes 393224 | tf_op jit(solution)/shard_map/ppermute | solution.py:30
  235.4 5.9 %copy-start.3 = (bf16[512,128]{0,1:T(8,128)(2,1)S(1)}, bf16[512,128]{0,1:T(8,128)(2,1)}, u32[]{:S(2)}) copy-start(bf16[512,128]{0,1:T(8,128)(2,1)} %get-tuple-element.24) | copy-start | bytes 393220
  244.0 7.8 %copy-start.6 = (s32[1,16]{1,0:T(1,128)S(1)}, s32[1,16]{1,0:T(1,128)}, u32[]{:S(2)}) copy-start(s32[1,16]{1,0:T(1,128)} %param.11) | copy-start | bytes 196
Sparse Core Ops, SparseCore 0:
  10.6 82.9 all-gather.2
  95.4 53.3 all-gather.4
  251.9 102.1 reduce-scatter.1
